TPU v7x, 32 devices: a whole 2x2x4 slice. The times are simulated.
32 devices in a mesh: clips: 2 (over x), seq: 16 (over z, y, core).
Axes of the slice: x: 2, y: 2, z: 4, core: 2. Of those that a mesh axis runs over, the one named last changes fastest.
Arguments:
- query_rows: bfloat16 [5120, 2560], P(('clips', 'seq')), parts along dimension 0, may hold values from -150 to 150
- key_rows: bfloat16 [5120, 2560], P(('clips', 'seq')), parts along dimension 0, may hold values from -7 to 7
- value_rows: bfloat16 [5120, 2560], P(('clips', 'seq')), parts along dimension 0, may hold values from -6 to 6
- target_rows: bfloat16 [5120, 2560], P(('clips', 'seq')), parts along dimension 0, may hold values from -6 to 6
- window: int32 [80, 10], replicated, may hold values from -1 to 79, as said below
Outputs:
- query_grad: bfloat16 [5120, 2560], P(('clips', 'seq')), parts along dimension 0
- key_grad: bfloat16 [5120, 2560], P(('clips', 'seq')), parts along dimension 0
- value_grad: bfloat16 [5120, 2560], P(('clips', 'seq')), parts along dimension 0
There are 2 independent parts, one for each index of `clips`. A program takes and returns all parts, laid end to end along the dimension named above; an argument that names none is the same for every part. Nothing has to cross between parts.
Inputs may be any that keep to these rules, and one draw needn't show every extreme that they name: `window`: entry 0 of row t is t. Entries 1 to 4 are distinct tiles below t and the others distinct tiles above t, each at most 5 tiles from t; an entry whose tile would fall outside the clip is -1.
All inputs are finite; a program needn't handle non-finite values.
Results may differ from a plain program's by a relative error of at most 0.029.
The roundings to bfloat16 on the way count: a program that leaves them out, or rounds other values in their place, can miss the bound.
Values may be sent and summed in bfloat16 or wider, within the bound.
A program may use at most 64 MiB of HBM per device.

v0:
```python
import jax
import jax.numpy as jnp
from jax import lax
from jax.sharding import PartitionSpec as P

HEADS = 20
HD = 128
BT = 32


def with_halo(cells, sides, width):
    for axis, dim in sides:
        count = lax.axis_size(axis)
        ends = count - 1
        head = lax.slice_in_dim(cells, 0, width, axis=dim)
        tail = lax.slice_in_dim(cells, cells.shape[dim] - width, cells.shape[dim], axis=dim)
        cells = jnp.concatenate(
            [
                lax.ppermute(tail, axis, [(i, (i + 1) % count) for i in range(ends)]),
                cells,
                lax.ppermute(head, axis, [((i + 1) % count, i) for i in range(ends)]),
            ],
            axis=dim,
        )
    return cells


def shifted(block, axis, distance):
    devices = range(lax.axis_size(axis))
    route = [(i - distance, i) for i in devices if i - distance in devices]
    return lax.ppermute(block, axis, route)


def tile_mask(table_rows, first_global, count):
    listed = first_global + jnp.arange(count, dtype=jnp.int32)
    matches = (table_rows[:, :, None] == listed[None, None, :]) & (table_rows[:, :, None] >= 0)
    hit = jnp.any(matches, axis=1)
    return jnp.repeat(jnp.repeat(hit, BT, axis=0), BT, axis=1)[None]


def grads_from(queries, out_grad, weights, weights_low, row_dot, values):
    score_scale = HD ** (-0.5)
    prob_grad = jnp.einsum("qhd,khd->hqk", out_grad, values, preferred_element_type=jnp.float32)
    score_grad = (weights * (prob_grad - row_dot) * score_scale).astype(jnp.bfloat16)
    key_part = jnp.einsum("hqk,qhd->khd", score_grad, queries, preferred_element_type=jnp.float32)
    value_part = jnp.einsum(
        "hqk,qhd->khd", weights_low, out_grad, preferred_element_type=jnp.float32
    )
    return (score_grad, key_part, value_part)


def shards(query_rows, key_rows, value_rows, target_rows, window):
    score_scale = HD ** (-0.5)
    row_count = query_rows.shape[0]
    tile_count = row_count // BT
    first_tile = lax.axis_index("seq") * tile_count
    stacked = jnp.stack([key_rows, value_rows])
    widened = with_halo(stacked, (("seq", 1),), row_count)
    key_ext = widened[0].reshape(3 * row_count, HEADS, HD)
    value_ext = widened[1].reshape(3 * row_count, HEADS, HD)
    padded = jnp.pad(window, ((tile_count, tile_count), (0, 0)), constant_values=-1)
    ext_table = lax.dynamic_slice_in_dim(padded, first_tile, 3 * tile_count, 0)
    own_table = ext_table[tile_count : 2 * tile_count]
    queries = query_rows.reshape(row_count, HEADS, HD)
    targets = target_rows.reshape(row_count, HEADS, HD)
    usable = tile_mask(own_table, first_tile - tile_count, 3 * tile_count)
    scores = (
        jnp.einsum("qhd,khd->hqk", queries, key_ext, preferred_element_type=jnp.float32)
        * score_scale
    )
    highest_score = jnp.max(jnp.where(usable, scores, -1e30), axis=-1, keepdims=True)
    denominator = jnp.sum(
        jnp.where(usable, jnp.exp(scores - highest_score), 0.0), axis=-1, keepdims=True
    )
    log_total = highest_score + jnp.log(denominator)
    weights = jnp.where(usable, jnp.exp(scores - log_total), 0.0)
    weights_low = weights.astype(jnp.bfloat16)
    output = jnp.einsum("hqk,khd->qhd", weights_low, value_ext, preferred_element_type=jnp.float32)
    out_grad = (output - targets.astype(jnp.float32)).astype(jnp.bfloat16)
    row_dot = jnp.transpose(jnp.sum(out_grad.astype(jnp.float32) * output, axis=-1), (1, 0))[
        ..., None
    ]
    score_grad, key_part, value_part = grads_from(
        queries, out_grad, weights, weights_low, row_dot, value_ext
    )
    query_grad = jnp.einsum("hqk,khd->qhd", score_grad, key_ext, preferred_element_type=jnp.float32)
    partials = jnp.stack([key_part, value_part])
    lower_side = partials[:, :row_count].astype(jnp.bfloat16)
    upper_side = partials[:, 2 * row_count :].astype(jnp.bfloat16)
    from_after = shifted(lower_side, "seq", -1)
    from_before = shifted(upper_side, "seq", 1)
    summed = (
        partials[:, row_count : 2 * row_count]
        + from_after.astype(jnp.float32)
        + from_before.astype(jnp.float32)
    )
    return (
        query_grad.reshape(row_count, HEADS * HD).astype(jnp.bfloat16),
        summed[0].reshape(row_count, HEADS * HD).astype(jnp.bfloat16),
        summed[1].reshape(row_count, HEADS * HD).astype(jnp.bfloat16),
    )


def solution(mesh):
    return jax.shard_map(
        shards,
        mesh=mesh,
        in_specs=(
            P(("clips", "seq"), None),
            P(("clips", "seq"), None),
            P(("clips", "seq"), None),
            P(("clips", "seq"), None),
            P(),
        ),
        out_specs=(P(("clips", "seq"), None), P(("clips", "seq"), None), P(("clips", "seq"), None)),
        check_vma=False,
    )
```

profile of v0, /device:TPU:11, one launch (start us, length us, event | category | flops | bytes accessed | tf_op | source)
XLA Modules:
  0.0 115.4 jit_solution(18103612517114052395)
XLA Ops:
  0.6 2.8 %pad_maximum_fusion.2 = bf16[2,160,2560]{2,1,0:T(8,128)(2,1)} fusion(bf16[1,160,2560]{2,1,0:T(8,128)(2,1)} %bitcast.94, bf16[1,160,2560]{2,1,0:T(8,128)(2,1)} %bitcast.96), kind=kLoop, calls=%fused_computation.24 | loop fusion | flops 819200 | bytes 3276800 | tf_op jit(solution)/shard_map/stack | solution.py:57
  3.4 2.6 %collective-permute-start.1 = (bf16[2,160,2560]{2,1,0:T(8,128)(2,1)}, bf16[2,160,2560]{2,1,0:T(8,128)(2,1)S(1)}, u32[]{:S(2)}, u32[]{:S(2)}) collective-permute-start(bf16[2,160,2560]{2,1,0:T(8,128)(2,1)} %pad_maximum_fusion.2), channel_id=1, source_target_pairs={{1,0},{2,1},{3,2},{4,3},{5,4},{6,5},{7,6},{8,7},{9,8},{10,9},{11,1... | collective-permute-start | bytes 4915208 | tf_op jit(solution)/shard_map/ppermute | solution.py:21
  6.0 3.0 %collective-permute-start = (bf16[2,160,2560]{2,1,0:T(8,128)(2,1)}, bf16[2,160,2560]{2,1,0:T(8,128)(2,1)}, u32[]{:S(2)}, u32[]{:S(2)}) collective-permute-start(bf16[2,160,2560]{2,1,0:T(8,128)(2,1)} %pad_maximum_fusion.2), channel_id=1, source_target_pairs={{0,1},{1,2},{2,3},{3,4},{4,5},{5,6},{6,7},{7,8},{8,9},{9,10},{10,1... | collective-permute-start | bytes 4915208 | tf_op jit(solution)/shard_map/ppermute | solution.py:19
  9.1 0.8 copy.59
  9.9 0.1 and_reduce_fusion
  10.0 0.1 copy.60
  10.2 0.1 reshape.37
  10.4 0.2 copy.61
  10.6 33.1 %collective-permute-done.1 = bf16[2,160,2560]{2,1,0:T(8,128)(2,1)S(1)} collective-permute-done((bf16[2,160,2560]{2,1,0:T(8,128)(2,1)}, bf16[2,160,2560]{2,1,0:T(8,128)(2,1)S(1)}, u32[]{:S(2)}, u32[]{:S(2)}) %collective-permute-start.1) | collective-permute-done | bytes 1638432 | tf_op jit(solution)/shard_map/ppermute | solution.py:21
  43.7 0.3 collective-permute-done
  44.0 2.1 %pad_maximum_fusion.1 = bf16[2,480,2560]{2,1,0:T(8,128)(2,1)S(1)} fusion(bf16[2,160,2560]{2,1,0:T(8,128)(2,1)S(1)} %collective-permute-done.1, bf16[1,160,2560]{2,1,0:T(8,128)(2,1)} %bitcast.95, bf16[1,160,2560]{2,1,0:T(8,128)(2,1)} %bitcast.97, bf16[2,160,2560]{2,1,0:T(8,128)(2,1)} %collective-permute-done), kind=kLoop, calls=%fused_computation.15 | loop fusion | flops 19660800 | bytes 9830400 | tf_op jit(solution)/shard_map/concatenate | solution.py:17
  46.1 1.8 %fusion.29 = (bf16[1,480,2560]{2,1,0:T(8,128)(2,1)S(1)}, bf16[1,480,2560]{2,1,0:T(8,128)(2,1)}) fusion(bf16[2,480,2560]{2,1,0:T(8,128)(2,1)S(1)} %pad_maximum_fusion.1), kind=kLoop, calls=%fused_computation.49 | loop fusion | bytes 9830400 | tf_op jit(solution)/shard_map/slice | solution.py:60
  47.9 2.6 %copy.64 = bf16[1,480,2560]{1,2,0:T(8,128)(2,1)} copy(bf16[1,480,2560]{2,1,0:T(8,128)(2,1)S(1)} %get-tuple-element.9) | data formatting | bytes 4915200 | tf_op jit(solution)/shard_map/slice | solution.py:60
  50.5 2.9 %copy.58 = bf16[1,480,2560]{1,2,0:T(8,128)(2,1)S(1)} copy(bf16[1,480,2560]{2,1,0:T(8,128)(2,1)} %get-tuple-element.10) | data formatting | bytes 4915200 | tf_op jit(solution)/shard_map/slice | solution.py:59
  53.4 1.4 %fusion.1 = (f32[20,160]{1,0:T(8,128)S(1)}, f32[20,480,160]{1,2,0:T(8,128)S(1)}) fusion(pred[160,480]{1,0:T(8,128)(4,1)S(1)} %copy.61, bf16[480,20,128]{0,2,1:T(8,128)(2,1)S(1)} %bitcast.90, bf16[160,2560]{1,0:T(8,128)(2,1)S(1)} %copy-done), kind=kOutput, calls=%fused_computation.7 | convolution fusion | flops 397820800 | bytes 9510400 | tf_op jit(solution)/shard_map/qhd,khd->hqk/dot_general | solution.py:68
  54.8 2.2 %fusion.4 = f32[20,160]{1,0:T(8,128)S(1)} fusion(f32[20,480,160]{1,2,0:T(8,128)S(1)} %get-tuple-element.14, f32[20,160]{1,0:T(8,128)S(1)} %get-tuple-element.13, pred[160,480]{1,0:T(8,128)(4,1)S(1)} %copy.61), kind=kLoop, calls=%fused_computation.10 | loop fusion | flops 6140800 | bytes 6246400 | tf_op jit(solution)/shard_map/reduce_sum | solution.py:72
  57.1 2.3 %fusion.13 = (f32[160,20]{0,1:T(8,128)S(1)}, bf16[160,20,128]{2,0,1:T(8,128)(2,1)S(1)}) fusion(bf16[480,20,128]{0,2,1:T(8,128)(2,1)S(1)} %bitcast.98, f32[20,480,160]{1,2,0:T(8,128)S(1)} %get-tuple-element.14, f32[20,160]{1,0:T(8,128)S(1)} %log_add_fusion, pred[160,480]{1,0:T(8,128)(4,1)S(1)} %copy.61, bf16[160,2560]{1,0:T(8,128)(2,1)S(1)} %copy-done.2), kind=kOutput, calls=%fused_computation.26 | convolution fusion | flops 401814400 | bytes 10342400 | tf_op jit(solution)/shard_map/hqk,khd->qhd/dot_general | solution.py:78
  59.4 3.1 %convolution_bitcast_fusion = f32[1,480,20,128]{3,1,2,0:T(8,128)S(1)} fusion(bf16[160,20,128]{2,0,1:T(8,128)(2,1)S(1)} %get-tuple-element.4, f32[20,480,160]{1,2,0:T(8,128)S(1)} %get-tuple-element.14, f32[20,160]{1,0:T(8,128)S(1)} %log_add_fusion, pred[160,480]{1,0:T(8,128)(4,1)S(1)} %copy.61), kind=kOutput, calls=%fused_computation.20 | convolution fusion | flops 399360000 | bytes 11968000 | tf_op jit(solution)/shard_map/hqk,qhd->khd/dot_general | solution.py:46
  62.5 2.6 %multiply_convert_fusion = bf16[20,160,480]{2,1,0:T(8,128)(2,1)S(1)} fusion(f32[20,480,160]{1,2,0:T(8,128)S(1)} %get-tuple-element.14, f32[20,160]{1,0:T(8,128)S(1)} %bitcast.102, f32[20,160]{1,0:T(8,128)S(1)} %log_add_fusion, pred[160,480]{1,0:T(8,128)(4,1)S(1)} %copy.61, bf16[160,20,128]{2,0,1:T(8,128)(2,1)S(1)} %get-tuple-element.4, ...), kind=kOutput, calls=%fused_computation.13 | convolution fusion | flops 403968000 | bytes 12595200 | tf_op jit(solution)/shard_map/qhd,khd->hqk/dot_general | solution.py:43
  65.1 1.6 %convolution_bitcast_fusion.1 = f32[1,480,20,128]{3,1,2,0:T(8,128)S(1)} fusion(bf16[20,160,480]{2,1,0:T(8,128)(2,1)S(1)} %multiply_convert_fusion, bf16[160,2560]{1,0:T(8,128)(2,1)S(1)} %copy-done), kind=kOutput, calls=%fused_computation.21 | convolution fusion | flops 393216000 | bytes 8806400 | tf_op jit(solution)/shard_map/hqk,qhd->khd/dot_general | solution.py:45
  66.7 3.0 %fusion = bf16[2,480,20,128]{3,1,2,0:T(8,128)(2,1)} fusion(f32[1,480,20,128]{3,1,2,0:T(8,128)S(1)} %convolution_bitcast_fusion, f32[1,480,20,128]{3,1,2,0:T(8,128)S(1)} %convolution_bitcast_fusion.1), kind=kLoop, calls=%fused_computation.3 | loop fusion | flops 2457600 | bytes 14745600 | tf_op jit(solution)/shard_map/convert.4
  69.8 2.1 %fusion.28 = (bf16[2,160,20,128]{3,1,2,0:T(8,128)(2,1)S(1)}, bf16[2,160,20,128]{3,1,2,0:T(8,128)(2,1)S(1)}) fusion(bf16[2,480,20,128]{3,1,2,0:T(8,128)(2,1)} %fusion), kind=kLoop, calls=%fused_computation.48 | loop fusion | bytes 6553600 | tf_op jit(solution)/shard_map/slice | solution.py:88
  71.9 2.1 %collective-permute-start.2 = (bf16[2,160,20,128]{3,1,2,0:T(8,128)(2,1)S(1)}, bf16[2,160,20,128]{3,1,2,0:T(8,128)(2,1)S(1)}, u32[]{:S(2)}, u32[]{:S(2)}) collective-permute-start(bf16[2,160,20,128]{3,1,2,0:T(8,128)(2,1)S(1)} %get-tuple-element.7), channel_id=1, source_target_pairs={{1,0},{2,1},{3,2},{4,3},{5,4},{6,5},{7,6},{8,7},{9,8},{10,9},{11,1... | collective-permute-start | bytes 4915208 | tf_op jit(solution)/shard_map/ppermute | solution.py:31
  74.0 4.4 %collective-permute-start.3 = (bf16[2,160,20,128]{3,1,2,0:T(8,128)(2,1)S(1)}, bf16[2,160,20,128]{3,1,2,0:T(8,128)(2,1)S(1)}, u32[]{:S(2)}, u32[]{:S(2)}) collective-permute-start(bf16[2,160,20,128]{3,1,2,0:T(8,128)(2,1)S(1)} %get-tuple-element.8), channel_id=1, source_target_pairs={{0,1},{1,2},{2,3},{3,4},{4,5},{5,6},{6,7},{7,8},{8,9},{9,10},{10,1... | collective-permute-start | bytes 4915208 | tf_op jit(solution)/shard_map/ppermute | solution.py:31
  78.4 1.1 fusion.14
  79.5 1.0 copy.97
  80.5 32.1 %collective-permute-done.2 = bf16[2,160,20,128]{3,1,2,0:T(8,128)(2,1)S(1)} collective-permute-done((bf16[2,160,20,128]{3,1,2,0:T(8,128)(2,1)S(1)}, bf16[2,160,20,128]{3,1,2,0:T(8,128)(2,1)S(1)}, u32[]{:S(2)}, u32[]{:S(2)}) %collective-permute-start.2) | collective-permute-done | bytes 1638432 | tf_op jit(solution)/shard_map/ppermute | solution.py:31
  112.7 0.6 fusion.11
  113.3 0.1 fusion.30
  113.4 0.3 copy.72
  113.7 0.3 copy.71
  114.1 1.3 %copy_bitcast_fusion = (bf16[160,2560]{1,0:T(8,128)(2,1)}, bf16[160,2560]{1,0:T(8,128)(2,1)}) fusion(bf16[20,8,20,128]{3,2,1,0:T(8,128)(2,1)S(1)} %bitcast.92, bf16[20,8,20,128]{3,2,1,0:T(8,128)(2,1)S(1)} %bitcast.93), kind=kLoop, calls=%fused_computation.30 | loop fusion | bytes 3276800 | tf_op jit(solution)/shard_map/convert_element_type | solution.py:100
  (12 shorter events, 0.2 us)
Async XLA Ops:
  0.6 52.8 %copy-start = (bf16[160,2560]{1,0:T(8,128)(2,1)S(1)}, bf16[160,2560]{1,0:T(8,128)(2,1)}, u32[]{:S(2)}) copy-start(bf16[160,2560]{1,0:T(8,128)(2,1)} %param.5) | copy-start | bytes 2457604
  3.4 40.3 %collective-permute-start.1 = (bf16[2,160,2560]{2,1,0:T(8,128)(2,1)}, bf16[2,160,2560]{2,1,0:T(8,128)(2,1)S(1)}, u32[]{:S(2)}, u32[]{:S(2)}) collective-permute-start(bf16[2,160,2560]{2,1,0:T(8,128)(2,1)} %pad_maximum_fusion.2), channel_id=1, source_target_pairs={{1,0},{2,1},{3,2},{4,3},{5,4},{6,5},{7,6},{8,7},{9,8},{10,9},{11,1... | collective-permute-start | bytes 4915208 | tf_op jit(solution)/shard_map/ppermute | solution.py:21
  6.0 38.0 %collective-permute-start = (bf16[2,160,2560]{2,1,0:T(8,128)(2,1)}, bf16[2,160,2560]{2,1,0:T(8,128)(2,1)}, u32[]{:S(2)}, u32[]{:S(2)}) collective-permute-start(bf16[2,160,2560]{2,1,0:T(8,128)(2,1)} %pad_maximum_fusion.2), channel_id=1, source_target_pairs={{0,1},{1,2},{2,3},{3,4},{4,5},{5,6},{6,7},{7,8},{8,9},{9,10},{10,1... | collective-permute-start | bytes 4915208 | tf_op jit(solution)/shard_map/ppermute | solution.py:19
  54.8 2.2 %copy-start.1 = (bf16[1,480,2560]{1,2,0:T(8,128)(2,1)S(1)}, bf16[1,480,2560]{1,2,0:T(8,128)(2,1)}, u32[]{:S(2)}) copy-start(bf16[1,480,2560]{1,2,0:T(8,128)(2,1)} %copy.64) | copy-start | bytes 7372804
  54.8 2.2 %copy-start.2 = (bf16[160,2560]{1,0:T(8,128)(2,1)S(1)}, bf16[160,2560]{1,0:T(8,128)(2,1)}, u32[]{:S(2)}) copy-start(bf16[160,2560]{1,0:T(8,128)(2,1)} %param.8) | copy-start | bytes 2457604
  71.9 40.8 %collective-permute-start.2 = (bf16[2,160,20,128]{3,1,2,0:T(8,128)(2,1)S(1)}, bf16[2,160,20,128]{3,1,2,0:T(8,128)(2,1)S(1)}, u32[]{:S(2)}, u32[]{:S(2)}) collective-permute-start(bf16[2,160,20,128]{3,1,2,0:T(8,128)(2,1)S(1)} %get-tuple-element.7), channel_id=1, source_target_pairs={{1,0},{2,1},{3,2},{4,3},{5,4},{6,5},{7,6},{8,7},{9,8},{10,9},{11,1... | collective-permute-start | bytes 4915208 | tf_op jit(solution)/shard_map/ppermute | solution.py:31
  74.0 38.7 %collective-permute-start.3 = (bf16[2,160,20,128]{3,1,2,0:T(8,128)(2,1)S(1)}, bf16[2,160,20,128]{3,1,2,0:T(8,128)(2,1)S(1)}, u32[]{:S(2)}, u32[]{:S(2)}) collective-permute-start(bf16[2,160,20,128]{3,1,2,0:T(8,128)(2,1)S(1)} %get-tuple-element.8), channel_id=1, source_target_pairs={{0,1},{1,2},{2,3},{3,4},{4,5},{5,6},{6,7},{7,8},{8,9},{9,10},{10,1... | collective-permute-start | bytes 4915208 | tf_op jit(solution)/shard_map/ppermute | solution.py:31
where the time goes:
time: 116 us; the launch traced here: 115 us
  waiting for transfers between devices  65.5 us (56%)
  local copies, waits for them, and re-layouts  13.9 us (12%)
  starting transfers between devices  12.1 us (10%)
  matrix products  12.1 us (10%)
  other arithmetic  10.8 us (9%)
    ppermute x1, waiting for transfers between devices, with_halo(): lax.ppermute(head, axis, [((i + 1) % count, i) for i in range(ends)])  33.1 us
    ppermute x2, waiting for transfers between devices, shifted(): return lax.ppermute(block, axis, route)  32.1 us
    ppermute x2, starting transfers between devices, shifted(): return lax.ppermute(block, axis, route)  6.51 us
    slice x2, local copies, waits for them, and re-layouts, shards(): value_ext = widened[1].reshape(3 * row_count, HEADS, HD)  4.37 us
    another operation x2, other arithmetic  3.61 us
    dot_general x1, matrix products, grads_from(): jnp.einsum('hqk,qhd->khd', weights_low, out_grad, preferred_element_type=...  3.12 us
    ppermute x1, starting transfers between devices, with_halo(): lax.ppermute(tail, axis, [(i, (i + 1) % count) for i in range(ends)])  3.05 us
    slice x1, local copies, waits for them, and re-layouts, shards(): key_ext = widened[0].reshape(3 * row_count, HEADS, HD)  2.95 us
  transfers between devices with their start and end apart: 4, of which 3 were waited for; matrix products, arithmetic and copies ran while one was open for 3% of the time, Pallas kernels for 0%

commit v1 on v0

v1 whole, which is shorter than its diff:
```python
import functools

import jax
import jax.numpy as jnp
from jax import lax
from jax.experimental import pallas as pl
from jax.experimental.pallas import tpu as pltpu
from jax.sharding import PartitionSpec as P

HEADS = 20
HD = 128
BT = 32
GROUP = 2
LOG2E = 1.4426950408889634


def dot(a, b, dims):
    return lax.dot_general(a, b, (dims, ((), ())), preferred_element_type=jnp.float32)


def kernel(
    count,
    win_ref,
    q_hbm,
    k_hbm,
    v_hbm,
    t_hbm,
    dq_ref,
    dk_ref,
    dv_ref,
    q_buf,
    t_buf,
    kx,
    vx,
    bias,
    acc_k,
    acc_v,
    part_k,
    part_v,
    got_k,
    got_v,
    local_sem,
    kv_send,
    kv_recv,
    part_send,
    part_recv,
):
    rows = q_buf.shape[0]
    tiles = rows // BT
    width = GROUP * HD
    groups = q_buf.shape[1] // width
    scale = HD ** (-0.5)
    me = lax.axis_index("seq")
    has = (me > 0, me < count - 1)
    peer = (me - 1, me + 1)
    place = (slice(0, rows), slice(2 * rows, 3 * rows))

    def columns(c):
        return pl.ds(pl.multiple_of(c * width, width), width)

    locals_ = [
        pltpu.make_async_copy(q_hbm, q_buf, local_sem.at[0]),
        pltpu.make_async_copy(k_hbm, kx.at[rows : 2 * rows], local_sem.at[1]),
        pltpu.make_async_copy(v_hbm, vx.at[rows : 2 * rows], local_sem.at[2]),
        pltpu.make_async_copy(t_hbm, t_buf, local_sem.at[3]),
    ]

    def kv_copy(side, arr, c, who):
        return pltpu.make_async_remote_copy(
            src_ref=(k_hbm, v_hbm)[arr].at[:, columns(c)],
            dst_ref=(kx, vx)[arr].at[place[1 - side], columns(c)],
            send_sem=kv_send.at[side, arr, c],
            recv_sem=kv_recv.at[1 - side, arr, c],
            device_id={"seq": who},
            device_id_type=pl.DeviceIdType.MESH,
        )

    def part_copy(side, arr, c, who):
        return pltpu.make_async_remote_copy(
            src_ref=(part_k, part_v)[arr].at[side, :, columns(c)],
            dst_ref=(got_k, got_v)[arr].at[1 - side, :, columns(c)],
            send_sem=part_send.at[side, arr, c],
            recv_sem=part_recv.at[1 - side, arr, c],
            device_id={"seq": who},
            device_id_type=pl.DeviceIdType.MESH,
        )

    barrier = pltpu.get_barrier_semaphore()
    for side in range(2):

        @pl.when(has[side])
        def _():
            pl.semaphore_signal(
                barrier,
                inc=1,
                device_id={"seq": peer[side]},
                device_id_type=pl.DeviceIdType.MESH,
            )

    for copy in locals_:
        copy.start()
    pl.semaphore_wait(barrier, has[0].astype(jnp.int32) + has[1].astype(jnp.int32))

    def send_group(c, carry):
        for side in range(2):

            @pl.when(has[side])
            def _():
                for arr in range(2):
                    kv_copy(side, arr, c, peer[side]).start()

        return carry

    lax.fori_loop(0, groups, send_group, 0)

    for side in range(2):

        @pl.when(jnp.logical_not(has[side]))
        def _():
            for buf in (kx, vx):
                buf[place[side]] = jnp.zeros((rows, buf.shape[1]), buf.dtype)
            for buf in (got_k, got_v):
                buf[side] = jnp.zeros(buf.shape[1:], buf.dtype)

    first = me * tiles
    listed = lax.broadcasted_iota(jnp.int32, (1, 3 * rows), 1) // BT + (first - tiles)
    for i in range(tiles):
        row_bias = jnp.full((1, 3 * rows), -1e30, jnp.float32)
        for j in range(win_ref.shape[1]):
            entry = win_ref[first + i, j]
            row_bias = jnp.where((listed == entry) & (listed >= 0), 0.0, row_bias)
        bias[i * BT : (i + 1) * BT] = jnp.broadcast_to(row_bias, (BT, 3 * rows))

    for copy in locals_:
        copy.wait()

    def one_head(col):
        cols = pl.ds(pl.multiple_of(col, HD), HD)
        q = q_buf[:, cols]
        k = kx[:, cols]
        v = vx[:, cols]
        s = dot(q, k, ((1,), (1,))) + bias[...]
        top = jnp.max(s, axis=-1, keepdims=True)
        e = jnp.exp2((s - top) * (scale * LOG2E))
        w = e * (1.0 / jnp.sum(e, axis=-1, keepdims=True))
        w_low = w.astype(jnp.bfloat16)
        out = dot(w_low, v, ((1,), (0,)))
        og = (out - t_buf[:, cols].astype(jnp.float32)).astype(jnp.bfloat16)
        rd = jnp.sum(og.astype(jnp.float32) * out, axis=-1, keepdims=True)
        dp = dot(og, v, ((1,), (1,)))
        ds = (w * (dp - rd) * scale).astype(jnp.bfloat16)
        dq_ref[:, cols] = dot(ds, k, ((1,), (0,))).astype(jnp.bfloat16)
        for parts, acc, left, right in (
            (part_k, acc_k, ds, q),
            (part_v, acc_v, w_low, og),
        ):
            g = dot(left, right, ((0,), (0,)))
            parts[0, :, cols] = g[:rows].astype(jnp.bfloat16)
            acc[:, cols] = g[rows : 2 * rows]
            parts[1, :, cols] = g[2 * rows :].astype(jnp.bfloat16)

    def compute_group(c, carry):
        for side in range(2):

            @pl.when(has[side])
            def _():
                for arr in range(2):
                    kv_copy(1 - side, arr, c, peer[side]).wait_recv()

        for g in range(GROUP):
            one_head(c * width + g * HD)
        for side in range(2):

            @pl.when(has[side])
            def _():
                for arr in range(2):
                    part_copy(side, arr, c, peer[side]).start()

        return carry

    lax.fori_loop(0, groups, compute_group, 0)

    def finish_group(c, carry):
        for side in range(2):

            @pl.when(has[side])
            def _():
                for arr in range(2):
                    part_copy(1 - side, arr, c, peer[side]).wait_recv()

        cols = columns(c)
        for acc, got, out_ref in ((acc_k, got_k, dk_ref), (acc_v, got_v, dv_ref)):
            out_ref[:, cols] = (
                acc[:, cols]
                + got[0, :, cols].astype(jnp.float32)
                + got[1, :, cols].astype(jnp.float32)
            ).astype(out_ref.dtype)
        return carry

    lax.fori_loop(0, groups, finish_group, 0)

    def drain_group(c, carry):
        for side in range(2):

            @pl.when(has[side])
            def _():
                for arr in range(2):
                    kv_copy(side, arr, c, peer[side]).wait_send()
                    part_copy(side, arr, c, peer[side]).wait_send()

        return carry

    lax.fori_loop(0, groups, drain_group, 0)


def shards(count, query_rows, key_rows, value_rows, target_rows, window):
    rows, cols = query_rows.shape
    groups = cols // (GROUP * HD)
    shape = jax.ShapeDtypeStruct((rows, cols), jnp.bfloat16)
    any_spec = pl.BlockSpec(memory_space=pl.ANY)
    vmem_spec = pl.BlockSpec(memory_space=pltpu.VMEM)
    return pl.pallas_call(
        functools.partial(kernel, count),
        out_shape=(shape, shape, shape),
        in_specs=[pl.BlockSpec(memory_space=pltpu.SMEM)] + [any_spec] * 4,
        out_specs=(vmem_spec, vmem_spec, vmem_spec),
        scratch_shapes=[
            pltpu.VMEM((rows, cols), jnp.bfloat16),
            pltpu.VMEM((rows, cols), jnp.bfloat16),
            pltpu.VMEM((3 * rows, cols), jnp.bfloat16),
            pltpu.VMEM((3 * rows, cols), jnp.bfloat16),
            pltpu.VMEM((rows, 3 * rows), jnp.float32),
            pltpu.VMEM((rows, cols), jnp.float32),
            pltpu.VMEM((rows, cols), jnp.float32),
            pltpu.VMEM((2, rows, cols), jnp.bfloat16),
            pltpu.VMEM((2, rows, cols), jnp.bfloat16),
            pltpu.VMEM((2, rows, cols), jnp.bfloat16),
            pltpu.VMEM((2, rows, cols), jnp.bfloat16),
            pltpu.SemaphoreType.DMA((4,)),
            pltpu.SemaphoreType.DMA((2, 2, groups)),
            pltpu.SemaphoreType.DMA((2, 2, groups)),
            pltpu.SemaphoreType.DMA((2, 2, groups)),
            pltpu.SemaphoreType.DMA((2, 2, groups)),
        ],
        compiler_params=pltpu.CompilerParams(
            collective_id=0, has_side_effects=True, vmem_limit_bytes=56 * 1024 * 1024
        ),
    )(window, query_rows, key_rows, value_rows, target_rows)


def solution(mesh):
    spec = P(("clips", "seq"), None)
    return jax.shard_map(
        functools.partial(shards, mesh.shape["seq"]),
        mesh=mesh,
        in_specs=(spec, spec, spec, spec, P()),
        out_specs=(spec, spec, spec),
        check_vma=False,
    )
```

time: 116 us -> 84.9 us (0.73)
  Pallas kernels: 0 us -> 77.9 us
  waiting for transfers between devices: 65.5 us -> 0 us
  matrix products: 12.1 us -> 0 us
  starting transfers between devices: 12.1 us -> 0 us
  other arithmetic: 10.8 us -> 0 us
  local copies, waits for them, and re-layouts: 13.9 us -> 5.9 us
    pallas_call x0 -> x1, Pallas kernels: none -> 77.9 us  [shards(): pl.pallas_call(functools.partial(kernel, count), out_shape=(shape, shape,...]
    ppermute x4 -> x0, waiting for transfers between devices: 65.5 us -> none  [the longest x1 33.1 us: with_halo(): lax.ppermute(head, axis, [((i + 1) % count, i) for i in range(ends)])]
    ppermute x4 -> x0, starting transfers between devices: 12.1 us -> none  [the longest x2 6.51 us: shifted(): return lax.ppermute(block, axis, route)]
    dot_general x6 -> x0, matrix products: 12.1 us -> none  [the longest x1 3.12 us: grads_from(): jnp.einsum('hqk,qhd->khd', weights_low, out_grad, preferred_element_type=...]
    slice x7 -> x0, local copies, waits for them, and re-layouts: 10.2 us -> none  [the longest x2 4.37 us: shards(): value_ext = widened[1].reshape(3 * row_count, HEADS, HD)]
    another operation x3 -> x0, other arithmetic: 6.4 us -> none
    unnamed x7 -> x8, local copies, waits for them, and re-layouts: 0.81 us -> 5.9 us
    convert_element_type x2 -> x0, local copies, waits for them, and re-layouts: 2.36 us -> none  [the longest x1 1.33 us: shards(): summed[1].reshape(row_count, HEADS * HD).astype(jnp.bfloat16)]
  transfers between devices with their start and end apart: 4 -> 0, of which waited for: 3 -> 0; matrix products, arithmetic and copies ran while one was open for 3% -> 0% of each run, Pallas kernels for 0% -> 0%
where the time goes in v1:
time: 84.9 us; the launch traced here: 84.5 us
  Pallas kernels  77.9 us (92%)
  local copies, waits for them, and re-layouts  5.9 us (7%)
    pallas_call x1, Pallas kernels, shards(): pl.pallas_call(functools.partial(kernel, count), out_shape=(shape, shape,...  77.9 us
    unnamed x8, local copies, waits for them, and re-layouts  5.9 us

profile of v1, /device:TPU:11, one launch (start us, length us, event | category | flops | bytes accessed | tf_op | source)
XLA Modules:
  0.0 84.5 jit_solution(18380450939111312917)
XLA Ops:
  0.6 1.4 %copy.8.win_ref = s32[80,10]{1,0:T(8,128)} copy(s32[80,10]{0,1:T(8,128)} %param.9) | data formatting | bytes 6400 | tf_op args[4]
  2.0 77.9 %shard_map.76 = (bf16[160,2560]{1,0:T(8,128)(2,1)}, bf16[160,2560]{1,0:T(8,128)(2,1)}, bf16[160,2560]{1,0:T(8,128)(2,1)}) custom-call(s32[80,10]{1,0:T(8,128)} %copy.8.win_ref, bf16[160,2560]{1,0:T(8,128)(2,1)} %q_hbm.1, bf16[160,2560]{1,0:T(8,128)(2,1)} %k_hbm.1, bf16[160,2560]{1,0:T(8,128)(2,1)} %v_hbm.1, bf16[160,2560]{1,0:T(8,128)(2,1)} %t_hbm.1), custom_call_target="tpu_custom_call" | custom-call | tf_op jit(solution)/shard_map/pallas_call | solution.py:222
  80.0 0.0 copy-start.1
  80.0 2.2 %copy.12 = bf16[160,2560]{1,0:T(8,128)(2,1)} copy(bf16[160,2560]{1,0:T(8,128)(2,1)} %get-tuple-element.6) | data formatting | bytes 1638400
  82.2 0.0 copy-done.1
  82.2 0.0 copy-start
  82.2 0.9 %copy.13 = bf16[160,2560]{1,0:T(8,128)(2,1)} copy(bf16[160,2560]{1,0:T(8,128)(2,1)S(1)} %copy-done.1) | data formatting | bytes 1638400
  83.1 0.5 copy-done
  83.6 0.9 %copy.14 = bf16[160,2560]{1,0:T(8,128)(2,1)} copy(bf16[160,2560]{1,0:T(8,128)(2,1)S(1)} %copy-done) | data formatting | bytes 1638400
Async XLA Ops:
  80.0 2.2 %copy-start.1 = (bf16[160,2560]{1,0:T(8,128)(2,1)S(1)}, bf16[160,2560]{1,0:T(8,128)(2,1)}, u32[]{:S(2)}) copy-start(bf16[160,2560]{1,0:T(8,128)(2,1)} %get-tuple-element.7) | copy-start | bytes 2457604
  82.2 1.4 %copy-start = (bf16[160,2560]{1,0:T(8,128)(2,1)S(1)}, bf16[160,2560]{1,0:T(8,128)(2,1)}, u32[]{:S(2)}) copy-start(bf16[160,2560]{1,0:T(8,128)(2,1)} %get-tuple-element.8) | copy-start | bytes 2457604

commit v2 on v1

v2 whole, which is shorter than its diff:
```python
import functools

import jax
import jax.numpy as jnp
from jax import lax
from jax.experimental import pallas as pl
from jax.experimental.pallas import tpu as pltpu
from jax.sharding import PartitionSpec as P

HEADS = 20
HD = 128
BT = 32
GROUP = 4
AHEAD = 3
LOG2E = 1.4426950408889634


def dot(a, b, dims):
    return lax.dot_general(a, b, (dims, ((), ())), preferred_element_type=jnp.float32)


def kernel(
    count,
    planes,
    win_ref,
    q_hbm,
    k_hbm,
    v_hbm,
    t_hbm,
    dq_ref,
    dk_ref,
    dv_ref,
    q_buf,
    t_buf,
    kx,
    vx,
    bias,
    acc_k,
    acc_v,
    part_k,
    part_v,
    got_k,
    got_v,
    relay,
    local_sem,
    sent,
    came,
    relay_send,
    relay_recv,
):
    rows = q_buf.shape[0]
    tiles = rows // BT
    width = GROUP * HD
    groups = q_buf.shape[1] // width
    scale = HD ** (-0.5)
    me = lax.axis_index("seq")
    has = (me > 0, me < count - 1)
    peer = (me - 1, me + 1)
    place = (slice(0, rows), slice(2 * rows, 3 * rows))

    per = 2 * planes
    depth = count // per
    z = me // per
    low = me % per == 0
    high = me % per == per - 1
    up = (GROUP * (depth - 1 - z) + depth // 2) // depth
    down = (GROUP * z + depth // 2) // depth
    relays = planes > 1
    mate = jnp.where(low, me + per - 1, me - per + 1)
    onward = jnp.where(low, me + per, me - per)
    detour = (low & has[0], high & has[1])
    detour_heads = (down, up)
    relay_heads = jnp.where(low, up, down)
    is_relay = (low & (z < depth - 1)) | (high & (z > 0))

    def columns(c):
        return pl.ds(pl.multiple_of(c * width, width), width)

    def head(c, g):
        return pl.ds(pl.multiple_of(c * width + g * HD, HD), HD)

    locals_ = [
        pltpu.make_async_copy(q_hbm, q_buf, local_sem.at[0]),
        pltpu.make_async_copy(k_hbm, kx.at[rows : 2 * rows], local_sem.at[1]),
        pltpu.make_async_copy(v_hbm, vx.at[rows : 2 * rows], local_sem.at[2]),
        pltpu.make_async_copy(t_hbm, t_buf, local_sem.at[3]),
    ]

    def remote(src, dst, send_sem, recv_sem, who):
        return pltpu.make_async_remote_copy(
            src_ref=src,
            dst_ref=dst,
            send_sem=send_sem,
            recv_sem=recv_sem,
            device_id={"seq": who},
            device_id_type=pl.DeviceIdType.MESH,
        )

    def source(side, kind, cols):
        if kind < 2:
            return (k_hbm, v_hbm)[kind].at[:, cols]
        return (part_k, part_v)[kind - 2].at[side, :, cols]

    def landing(side, kind, cols):
        if kind < 2:
            return (kx, vx)[kind].at[place[side], cols]
        return (got_k, got_v)[kind - 2].at[side, :, cols]

    def group_copy(side, kind, c, who):
        cols = columns(c)
        return remote(
            source(side, kind, cols),
            landing(1 - side, kind, cols),
            sent.at[side, kind, c],
            came.at[1 - side, kind, c],
            who,
        )

    def head_copy(side, kind, c, g, who):
        cols = head(c, g)
        return remote(
            source(side, kind, cols),
            landing(1 - side, kind, cols),
            sent.at[side, kind, c],
            came.at[1 - side, kind, c],
            who,
        )

    def mate_copy(side, kind, c, g):
        cols = head(c, g)
        return remote(
            source(side, kind, cols),
            relay.at[kind, :, cols],
            sent.at[side, kind, c],
            relay_recv.at[kind, c * GROUP + g],
            mate,
        )

    def onward_copy(side, kind, c, g):
        cols = head(c, g)
        return remote(
            relay.at[kind, :, cols],
            landing(1 - side, kind, cols),
            relay_send.at[kind, c * GROUP + g],
            came.at[1 - side, kind, c],
            onward,
        )

    def send(kinds, c):
        for side in range(2):
            if not relays:

                @pl.when(has[side])
                def _():
                    for kind in kinds:
                        group_copy(side, kind, c, peer[side]).start()

                continue

            @pl.when(has[side] & jnp.logical_not(detour[side]))
            def _():
                for kind in kinds:
                    group_copy(side, kind, c, peer[side]).start()

            @pl.when(detour[side])
            def _():
                for g in range(GROUP):

                    @pl.when(g < detour_heads[side])
                    def _():
                        for kind in kinds:
                            mate_copy(side, kind, c, g).start()

                    @pl.when(g >= detour_heads[side])
                    def _():
                        for kind in kinds:
                            head_copy(side, kind, c, g, peer[side]).start()

    def await_group(kinds, c):
        for side in range(2):

            @pl.when(has[side])
            def _():
                for kind in kinds:
                    group_copy(1 - side, kind, c, peer[side]).wait_recv()

    def forward(kinds, c, finish=False):
        if not relays:
            return
        for side, end in ((1, low), (0, high)):

            @pl.when(end & is_relay)
            def _():
                for g in range(GROUP):

                    @pl.when(g < relay_heads)
                    def _():
                        for kind in kinds:
                            if finish:
                                onward_copy(side, kind, c, g).wait_send()
                            else:
                                mate_copy(side, kind, c, g).wait_recv()
                                onward_copy(side, kind, c, g).start()

    barrier = pltpu.get_barrier_semaphore()

    def greet(who):
        pl.semaphore_signal(
            barrier, inc=1, device_id={"seq": who}, device_id_type=pl.DeviceIdType.MESH
        )

    greeted = has[0].astype(jnp.int32) + has[1].astype(jnp.int32)
    for side in range(2):

        @pl.when(has[side])
        def _():
            greet(peer[side])

    if relays:
        end = low | high
        before, after = end & (z > 0), end & (z < depth - 1)
        for cond, who in ((end, mate), (before, me - per), (after, me + per)):

            @pl.when(cond)
            def _():
                greet(who)

            greeted = greeted + cond.astype(jnp.int32)
    for copy in locals_:
        copy.start()
    pl.semaphore_wait(barrier, greeted)

    def send_group(c, carry):
        send((0, 1), c)
        return carry

    lax.fori_loop(0, AHEAD, send_group, 0)

    for side in range(2):

        @pl.when(jnp.logical_not(has[side]))
        def _():
            for buf in (kx, vx):
                buf[place[side]] = jnp.zeros((rows, buf.shape[1]), buf.dtype)
            for buf in (got_k, got_v):
                buf[side] = jnp.zeros(buf.shape[1:], buf.dtype)

    first = me * tiles
    listed = lax.broadcasted_iota(jnp.int32, (1, 3 * rows), 1) // BT + (first - tiles)
    for i in range(tiles):
        row_bias = jnp.full((1, 3 * rows), -1e30, jnp.float32)
        for j in range(win_ref.shape[0]):
            entry = win_ref[j, first + i]
            row_bias = jnp.where((listed == entry) & (listed >= 0), 0.0, row_bias)
        bias[i * BT : (i + 1) * BT] = jnp.broadcast_to(row_bias, (BT, 3 * rows))

    for copy in locals_:
        copy.wait()

    def one_head(col):
        cols = pl.ds(pl.multiple_of(col, HD), HD)
        q = q_buf[:, cols]
        k = kx[:, cols]
        v = vx[:, cols]
        s = dot(q, k, ((1,), (1,))) + bias[...]
        top = jnp.max(s, axis=-1, keepdims=True)
        e = jnp.exp2((s - top) * (scale * LOG2E))
        w = e * (1.0 / jnp.sum(e, axis=-1, keepdims=True))
        w_low = w.astype(jnp.bfloat16)
        out = dot(w_low, v, ((1,), (0,)))
        og = (out - t_buf[:, cols].astype(jnp.float32)).astype(jnp.bfloat16)
        rd = jnp.sum(og.astype(jnp.float32) * out, axis=-1, keepdims=True)
        dp = dot(og, v, ((1,), (1,)))
        ds = (w * (dp - rd) * scale).astype(jnp.bfloat16)
        dq_ref[:, cols] = dot(ds, k, ((1,), (0,))).astype(jnp.bfloat16)
        for parts, acc, left, right in (
            (part_k, acc_k, ds, q),
            (part_v, acc_v, w_low, og),
        ):
            g = dot(left, right, ((0,), (0,)))
            parts[0, :, cols] = g[:rows].astype(jnp.bfloat16)
            acc[:, cols] = g[rows : 2 * rows]
            parts[1, :, cols] = g[2 * rows :].astype(jnp.bfloat16)

    def compute_group(c, carry):
        forward((0, 1), c)
        await_group((0, 1), c)
        for g in range(GROUP):
            one_head(c * width + g * HD)
        send((2, 3), c)
        if AHEAD < groups:

            @pl.when(c + AHEAD < groups)
            def _():
                send((0, 1), c + AHEAD)

        @pl.when(c > 0)
        def _():
            forward((2, 3), c - 1)

        return carry

    lax.fori_loop(0, groups, compute_group, 0)
    forward((2, 3), groups - 1)

    def finish_group(c, carry):
        await_group((2, 3), c)
        cols = columns(c)
        for acc, got, out_ref in ((acc_k, got_k, dk_ref), (acc_v, got_v, dv_ref)):
            out_ref[:, cols] = (
                acc[:, cols]
                + got[0, :, cols].astype(jnp.float32)
                + got[1, :, cols].astype(jnp.float32)
            ).astype(out_ref.dtype)
        return carry

    lax.fori_loop(0, groups, finish_group, 0)

    def drain_group(c, carry):
        for side in range(2):

            @pl.when(has[side])
            def _():
                for kind in range(4):
                    group_copy(side, kind, c, peer[side]).wait_send()

        forward((0, 1, 2, 3), c, finish=True)
        return carry

    lax.fori_loop(0, groups, drain_group, 0)


def shards(count, planes, query_rows, key_rows, value_rows, target_rows, window):
    rows, cols = query_rows.shape
    groups = cols // (GROUP * HD)
    shape = jax.ShapeDtypeStruct((rows, cols), jnp.bfloat16)
    any_spec = pl.BlockSpec(memory_space=pl.ANY)
    vmem_spec = pl.BlockSpec(memory_space=pltpu.VMEM)
    return pl.pallas_call(
        functools.partial(kernel, count, planes),
        out_shape=(shape, shape, shape),
        in_specs=[pl.BlockSpec(memory_space=pltpu.SMEM)] + [any_spec] * 4,
        out_specs=(vmem_spec, vmem_spec, vmem_spec),
        scratch_shapes=[
            pltpu.VMEM((rows, cols), jnp.bfloat16),
            pltpu.VMEM((rows, cols), jnp.bfloat16),
            pltpu.VMEM((3 * rows, cols), jnp.bfloat16),
            pltpu.VMEM((3 * rows, cols), jnp.bfloat16),
            pltpu.VMEM((rows, 3 * rows), jnp.float32),
            pltpu.VMEM((rows, cols), jnp.float32),
            pltpu.VMEM((rows, cols), jnp.float32),
            pltpu.VMEM((2, rows, cols), jnp.bfloat16),
            pltpu.VMEM((2, rows, cols), jnp.bfloat16),
            pltpu.VMEM((2, rows, cols), jnp.bfloat16),
            pltpu.VMEM((2, rows, cols), jnp.bfloat16),
            pltpu.VMEM((4, rows, cols), jnp.bfloat16),
            pltpu.SemaphoreType.DMA((4,)),
            pltpu.SemaphoreType.DMA((2, 4, groups)),
            pltpu.SemaphoreType.DMA((2, 4, groups)),
            pltpu.SemaphoreType.DMA((4, HEADS)),
            pltpu.SemaphoreType.DMA((4, HEADS)),
        ],
        compiler_params=pltpu.CompilerParams(
            collective_id=0, has_side_effects=True, vmem_limit_bytes=56 * 1024 * 1024
        ),
    )(window.T, query_rows, key_rows, value_rows, target_rows)


def solution(mesh):
    spec = P(("clips", "seq"), None)
    return jax.shard_map(
        functools.partial(shards, mesh.shape["seq"], 4 // mesh.shape["clips"]),
        mesh=mesh,
        in_specs=(spec, spec, spec, spec, P()),
        out_specs=(spec, spec, spec),
        check_vma=False,
    )
```

time: 84.9 us -> 75.8 us (0.89)
  Pallas kernels: 77.9 us -> 69.6 us
  local copies, waits for them, and re-layouts: 5.9 us -> 4.5 us
    pallas_call x1, Pallas kernels: 77.9 us -> 69.6 us  [shards(): pl.pallas_call(functools.partial(kernel, count, planes), out_shape=(shape...]
    unnamed x8 -> x7, local copies, waits for them, and re-layouts: 5.9 us -> 4.5 us
where the time goes in v2:
time: 75.8 us; the launch traced here: 74.7 us
  Pallas kernels  69.6 us (92%)
  local copies, waits for them, and re-layouts  4.5 us (6%)
    pallas_call x1, Pallas kernels, shards(): pl.pallas_call(functools.partial(kernel, count, planes), out_shape=(shape...  69.6 us
    unnamed x7, local copies, waits for them, and re-layouts  4.5 us

profile of v2, /device:TPU:11, one launch (start us, length us, event | category | flops | bytes accessed | tf_op | source)
XLA Modules:
  0.0 74.7 jit_solution(11122985091549171025)
XLA Ops:
  0.6 69.6 %shard_map.76 = (bf16[160,2560]{1,0:T(8,128)(2,1)}, bf16[160,2560]{1,0:T(8,128)(2,1)}, bf16[160,2560]{1,0:T(8,128)(2,1)}) custom-call(s32[10,80]{1,0:T(8,128)} %bitcast.1, bf16[160,2560]{1,0:T(8,128)(2,1)} %q_hbm.1, bf16[160,2560]{1,0:T(8,128)(2,1)} %k_hbm.1, bf16[160,2560]{1,0:T(8,128)(2,1)} %v_hbm.1, bf16[160,2560]{1,0:T(8,128)(2,1)} %t_hbm.1), custom_call_target="tpu_custom_call" | custom-call | tf_op jit(solution)/shard_map/pallas_call | solution.py:339
  70.2 0.0 copy-start.1
  70.2 2.2 %copy.11 = bf16[160,2560]{1,0:T(8,128)(2,1)} copy(bf16[160,2560]{1,0:T(8,128)(2,1)} %get-tuple-element.6) | data formatting | bytes 1638400
  72.4 0.0 copy-done.1
  72.4 0.0 copy-start
  72.4 0.9 %copy.12 = bf16[160,2560]{1,0:T(8,128)(2,1)} copy(bf16[160,2560]{1,0:T(8,128)(2,1)S(1)} %copy-done.1) | data formatting | bytes 1638400
  73.3 0.5 copy-done
  73.9 0.9 %copy.13 = bf16[160,2560]{1,0:T(8,128)(2,1)} copy(bf16[160,2560]{1,0:T(8,128)(2,1)S(1)} %copy-done) | data formatting | bytes 1638400
Async XLA Ops:
  70.2 2.2 %copy-start.1 = (bf16[160,2560]{1,0:T(8,128)(2,1)S(1)}, bf16[160,2560]{1,0:T(8,128)(2,1)}, u32[]{:S(2)}) copy-start(bf16[160,2560]{1,0:T(8,128)(2,1)} %get-tuple-element.7) | copy-start | bytes 2457604
  72.4 1.4 %copy-start = (bf16[160,2560]{1,0:T(8,128)(2,1)S(1)}, bf16[160,2560]{1,0:T(8,128)(2,1)}, u32[]{:S(2)}) copy-start(bf16[160,2560]{1,0:T(8,128)(2,1)} %get-tuple-element.8) | copy-start | bytes 2457604

commit v3 on v2

--- a/solution.py
+++ b/solution.py
@@ -12,6 +12,8 @@
 BT = 32
 GROUP = 4
 AHEAD = 3
+LAG = 2
+SHARES = 4
 LOG2E = 1.4426950408889634
 
 
@@ -63,8 +65,8 @@
     z = me // per
     low = me % per == 0
     high = me % per == per - 1
-    up = (GROUP * (depth - 1 - z) + depth // 2) // depth
-    down = (GROUP * z + depth // 2) // depth
+    up = (SHARES * (depth - 1 - z) + depth // 2) // depth
+    down = (SHARES * z + depth // 2) // depth
     relays = planes > 1
     mate = jnp.where(low, me + per - 1, me - per + 1)
     onward = jnp.where(low, me + per, me - per)
@@ -75,6 +77,10 @@
 
     def columns(c):
         return pl.ds(pl.multiple_of(c * width, width), width)
+
+    def rank(c, g):
+        h = c * GROUP + g
+        return h % 2 * 2 + h // 2 % 2
 
     def head(c, g):
         return pl.ds(pl.multiple_of(c * width + g * HD, HD), HD)
@@ -166,12 +172,12 @@
             def _():
                 for g in range(GROUP):
 
-                    @pl.when(g < detour_heads[side])
+                    @pl.when(rank(c, g) < detour_heads[side])
                     def _():
                         for kind in kinds:
                             mate_copy(side, kind, c, g).start()
 
-                    @pl.when(g >= detour_heads[side])
+                    @pl.when(rank(c, g) >= detour_heads[side])
                     def _():
                         for kind in kinds:
                             head_copy(side, kind, c, g, peer[side]).start()
@@ -193,7 +199,7 @@
             def _():
                 for g in range(GROUP):
 
-                    @pl.when(g < relay_heads)
+                    @pl.when(rank(c, g) < relay_heads)
                     def _():
                         for kind in kinds:
                             if finish:
@@ -283,6 +289,10 @@
             parts[1, :, cols] = g[2 * rows :].astype(jnp.bfloat16)
 
     def compute_group(c, carry):
+        @pl.when(c >= LAG)
+        def _():
+            forward((2, 3), c - LAG)
+
         forward((0, 1), c)
         await_group((0, 1), c)
         for g in range(GROUP):
@@ -294,14 +304,15 @@
             def _():
                 send((0, 1), c + AHEAD)
 
-        @pl.when(c > 0)
-        def _():
-            forward((2, 3), c - 1)
-
         return carry
 
     lax.fori_loop(0, groups, compute_group, 0)
-    forward((2, 3), groups - 1)
+
+    def forward_group(c, carry):
+        forward((2, 3), c)
+        return carry
+
+    lax.fori_loop(max(groups - LAG, 0), groups, forward_group, 0)
 
     def finish_group(c, carry):
         await_group((2, 3), c)
@@ -330,15 +341,24 @@
     lax.fori_loop(0, groups, drain_group, 0)
 
 
+def write_out(*refs):
+    copies = [pltpu.make_async_copy(refs[i], refs[i + 3], refs[6].at[i]) for i in range(3)]
+    for copy in copies:
+        copy.start()
+    for copy in copies:
+        copy.wait()
+
+
 def shards(count, planes, query_rows, key_rows, value_rows, target_rows, window):
     rows, cols = query_rows.shape
     groups = cols // (GROUP * HD)
     shape = jax.ShapeDtypeStruct((rows, cols), jnp.bfloat16)
-    any_spec = pl.BlockSpec(memory_space=pl.ANY)
+    any_spec = pl.BlockSpec(memory_space=pltpu.HBM)
     vmem_spec = pl.BlockSpec(memory_space=pltpu.VMEM)
-    return pl.pallas_call(
+    near = pltpu.VMEM((rows, cols), jnp.bfloat16)
+    grads = pl.pallas_call(
         functools.partial(kernel, count, planes),
-        out_shape=(shape, shape, shape),
+        out_shape=(near, near, near),
         in_specs=[pl.BlockSpec(memory_space=pltpu.SMEM)] + [any_spec] * 4,
         out_specs=(vmem_spec, vmem_spec, vmem_spec),
         scratch_shapes=[
@@ -361,9 +381,17 @@
             pltpu.SemaphoreType.DMA((4, HEADS)),
         ],
         compiler_params=pltpu.CompilerParams(
-            collective_id=0, has_side_effects=True, vmem_limit_bytes=56 * 1024 * 1024
+            collective_id=0, has_side_effects=True, vmem_limit_bytes=57 * 1024 * 1024
         ),
     )(window.T, query_rows, key_rows, value_rows, target_rows)
+    grads = [pltpu.with_memory_space_constraint(grad, pltpu.VMEM) for grad in grads]
+    return pl.pallas_call(
+        write_out,
+        out_shape=(shape, shape, shape),
+        in_specs=[vmem_spec] * 3,
+        out_specs=(any_spec, any_spec, any_spec),
+        scratch_shapes=[pltpu.SemaphoreType.DMA((3,))],
+    )(*grads)
 
 
 def solution(mesh):

time: 75.8 us -> 71.2 us (0.939)
  local copies, waits for them, and re-layouts: 4.5 us -> 0 us
    unnamed x7 -> x0, local copies, waits for them, and re-layouts: 4.5 us -> none
    pallas_call x1 -> x2, Pallas kernels: 69.6 us -> 69.5 us  [the longest x1 68.1 us: shards(): pl.pallas_call(functools.partial(kernel, count, planes), out_shape=(near,...]
where the time goes in v3:
time: 71.2 us; the launch traced here: 70.2 us
  Pallas kernels  69.5 us (98%)
    pallas_call x1, Pallas kernels, shards(): pl.pallas_call(functools.partial(kernel, count, planes), out_shape=(near,...  68.1 us
    pallas_call x1, Pallas kernels, shards(): pl.pallas_call(write_out, out_shape=(shape, shape, shape), in_specs=[vmem...  1.46 us

profile of v3, /device:TPU:11, one launch (start us, length us, event | category | flops | bytes accessed | tf_op | source)
XLA Modules:
  0.0 70.2 jit_solution(10356542184232603750)
XLA Ops:
  0.6 68.1 %shard_map.76 = (bf16[160,2560]{1,0:T(8,128)(2,1)S(1)}, bf16[160,2560]{1,0:T(8,128)(2,1)S(1)}, bf16[160,2560]{1,0:T(8,128)(2,1)S(1)}) custom-call(s32[10,80]{1,0:T(8,128)} %bitcast.1, bf16[160,2560]{1,0:T(8,128)(2,1)} %q_hbm.1, bf16[160,2560]{1,0:T(8,128)(2,1)} %k_hbm.1, bf16[160,2560]{1,0:T(8,128)(2,1)} %v_hbm.1, bf16[160,2560]{1,0:T(8,128)(2,1)} %t_hbm.1), custom_call_target="tpu_custom_call" | custom-call | tf_op jit(solution)/shard_map/pallas_call | solution.py:359
  68.7 1.5 %shard_map.77 = (bf16[160,2560]{1,0:T(8,128)(2,1)}, bf16[160,2560]{1,0:T(8,128)(2,1)}, bf16[160,2560]{1,0:T(8,128)(2,1)}) custom-call(bf16[160,2560]{1,0:T(8,128)(2,1)S(1)} %get-tuple-element.6.refs_0_, bf16[160,2560]{1,0:T(8,128)(2,1)S(1)} %get-tuple-element.7.refs_1_, bf16[160,2560]{1,0:T(8,128)(2,1)S(1)} %get-tuple-element.8.refs_2_), custom_call_target="tpu_custom_call" | custom-call | tf_op jit(solution)/shard_map/pallas_call | solution.py:388
